TPU v7x, 32 devices: a whole 2x2x4 slice. The times are simulated.
32 devices in a mesh: groups: 2 (over y), replica: 1, da: 4 (over x, core), db: 4 (over z).
Axes of the slice: x: 2, y: 2, z: 4, core: 2. Of those that a mesh axis runs over, the one named last changes fastest.
Arguments:
- tokens: bfloat16 [4096, 1024], P(('groups', 'replica', 'da', 'db')), parts along dimension 0, may hold values from -6 to 6
- grad_out: bfloat16 [4096, 1024], P(('groups', 'replica', 'da', 'db')), parts along dimension 0, may hold values from -3 to 3
- routes: int32 [4096, 8], P(('groups', 'replica', 'da', 'db')), parts along dimension 0, may hold values from 0 to 15, as said below
- gates: bfloat16 [4096, 8], P(('groups', 'replica', 'da', 'db')), parts along dimension 0, may hold values from 0.019897461 to 0.5
- w_gate_up: bfloat16 [16, 1024, 768], P(('da', 'db'), 'replica'), may hold values from -0.1875 to 0.1875
- w_down: bfloat16 [16, 384, 1024], P(('da', 'db'), 'replica'), may hold values from -0.3125 to 0.3125
Outputs:
- token_grads: bfloat16 [4096, 1024], P(('groups', 'replica', 'da', 'db')), parts along dimension 0
- gate_grads: bfloat16 [4096, 8], P(('groups', 'replica', 'da', 'db')), parts along dimension 0
- gate_up_grads: bfloat16 [32, 1024, 768], P(('groups', 'da', 'db'), 'replica'), parts along dimension 0
- down_grads: bfloat16 [32, 384, 1024], P(('groups', 'da', 'db'), 'replica'), parts along dimension 0
There are 2 independent parts, one for each index of `groups`. A program takes and returns all parts, laid end to end along the dimension named above; an argument that names none is the same for every part. Nothing has to cross between parts.
Inputs may be any that keep to these rules, and one draw needn't show every extreme that they name: `routes`: each token names 8 different experts. In every aligned block of 2 consecutive tokens, each expert is named exactly once, so the tokens of one device name every expert exactly 64 times.
All inputs are finite; a program needn't handle non-finite values.
Results may differ from a plain program's by a relative error of at most 0.0085.
Values may be sent and summed in bfloat16 or wider, within the bound.
A program may use at most 64 MiB of HBM per device.

v0:
```python
import jax
import jax.numpy as jnp
from jax import lax
from jax.sharding import PartitionSpec as P


def silu_parts(projected):
    sigmoid = jax.nn.sigmoid(projected)
    return (projected * sigmoid, sigmoid * (1.0 + projected * (1.0 - sigmoid)))


def body(tokens, grad_out, routes, gates, w_gate_up, w_down):
    local_tokens, features = tokens.shape
    top_count = routes.shape[1]
    hidden_units = w_gate_up.shape[2] // 2
    first_size = lax.axis_size("da")
    second_size = lax.axis_size("db")
    experts = first_size * second_size
    per_round = experts // top_count
    rounds = local_tokens // per_round
    expert_ids = lax.broadcasted_iota(jnp.int32, (1, 1, 1, experts), 3)
    matches = routes.reshape(rounds, per_round, top_count, 1) == expert_ids
    gate_values = gates.reshape(rounds, per_round, top_count, 1).astype(jnp.float32)
    gate_table = jnp.sum(jnp.where(matches, gate_values, 0.0), axis=(1, 2)).astype(jnp.bfloat16)
    chosen = jnp.any(matches, axis=2).astype(jnp.bfloat16)
    input_send = jnp.einsum(
        "rge,rgd->red",
        chosen,
        tokens.reshape(rounds, per_round, features),
        preferred_element_type=jnp.float32,
    ).astype(jnp.bfloat16)
    upstream_send = jnp.einsum(
        "rge,rgd->red",
        chosen,
        grad_out.reshape(rounds, per_round, features),
        preferred_element_type=jnp.float32,
    ).astype(jnp.bfloat16)
    input_recv, upstream_recv, gate_recv = (
        lax.all_to_all(input_send, ("da", "db"), split_axis=1, concat_axis=1, tiled=True),
        lax.all_to_all(upstream_send, ("da", "db"), split_axis=1, concat_axis=1, tiled=True),
        lax.all_to_all(gate_table, ("da", "db"), split_axis=1, concat_axis=1, tiled=True),
    )
    input_rows = input_recv.reshape(-1, features)
    upstream_rows = upstream_recv.reshape(-1, features)
    gate_rows = gate_recv.reshape(-1, 1).astype(jnp.float32)
    w_in, w_out = (
        lax.all_gather(w_gate_up[0], "replica", axis=0, tiled=True),
        lax.all_gather(w_down[0], "replica", axis=0, tiled=True),
    )
    projected = jnp.dot(input_rows, w_in, preferred_element_type=jnp.float32)
    back_raw = jnp.einsum("rd,fd->rf", upstream_rows, w_out, preferred_element_type=jnp.float32)
    gate_part = projected[:, :hidden_units]
    up_part = projected[:, hidden_units:]
    activated, derivative = silu_parts(gate_part)
    hidden = (activated * up_part).astype(jnp.bfloat16)
    gate_scores = jnp.sum(hidden.astype(jnp.float32) * back_raw, axis=1).astype(jnp.bfloat16)
    back_hidden = gate_rows * back_raw
    grad_projected = jnp.concatenate(
        [back_hidden * up_part * derivative, back_hidden * activated], axis=1
    ).astype(jnp.bfloat16)
    scaled_upstream = (gate_rows * upstream_rows.astype(jnp.float32)).astype(jnp.bfloat16)
    input_grads = jnp.einsum("rf,df->rd", grad_projected, w_in, preferred_element_type=jnp.float32)
    input_grads = input_grads.astype(jnp.bfloat16).reshape(rounds, experts, features)
    score_back = gate_scores.reshape(rounds, experts)
    returned, score_ret = (
        lax.all_to_all(input_grads, ("da", "db"), split_axis=1, concat_axis=1, tiled=True),
        lax.all_to_all(score_back, ("da", "db"), split_axis=1, concat_axis=1, tiled=True),
    )
    score_ret = score_ret.reshape(rounds, 1, 1, experts).astype(jnp.float32)
    token_grads = (
        jnp.einsum("rge,red->rgd", chosen, returned, preferred_element_type=jnp.float32)
        .astype(jnp.bfloat16)
        .reshape(local_tokens, features)
    )
    gate_grads = (
        jnp.sum(jnp.where(matches, score_ret, 0.0), axis=3)
        .astype(jnp.bfloat16)
        .reshape(local_tokens, top_count)
    )
    columns = input_rows
    grad_in = lax.psum_scatter(
        jnp.einsum("rd,rf->df", columns, grad_projected, preferred_element_type=jnp.float32).astype(
            jnp.bfloat16
        ),
        "replica",
        scatter_dimension=0,
        tiled=True,
    )
    columns = hidden
    grad_down = lax.psum_scatter(
        jnp.einsum(
            "rf,rd->fd", columns, scaled_upstream, preferred_element_type=jnp.float32
        ).astype(jnp.bfloat16),
        "replica",
        scatter_dimension=0,
        tiled=True,
    )
    return (token_grads, gate_grads, grad_in[None], grad_down[None])


def solution(mesh):
    placed = (
        P(("groups", "replica", "da", "db"), None),
        P(("groups", "replica", "da", "db"), None),
        P(("groups", "replica", "da", "db"), None),
        P(("groups", "replica", "da", "db"), None),
        P(("da", "db"), "replica", None),
        P(("da", "db"), "replica", None),
    )
    return jax.shard_map(
        body,
        mesh=mesh,
        in_specs=placed,
        out_specs=(
            P(("groups", "replica", "da", "db"), None),
            P(("groups", "replica", "da", "db"), None),
            P(("groups", "da", "db"), "replica", None),
            P(("groups", "da", "db"), "replica", None),
        ),
        check_vma=False,
    )
```

profile of v0, /device:TPU:0, one launch (start us, length us, event | category | flops | bytes accessed | tf_op | source)
XLA Modules:
  0.0 206.5 jit_solution(12314356661567460310)
XLA Ops:
  0.6 0.9 copy.56
  1.7 0.1 copy.70
  1.8 1.1 reshape.88
  2.8 0.8 convolution_convert_fusion
  3.6 2.5 %copy.67 = bf16[64,16,1024]{2,0,1:T(8,128)(2,1)} copy(bf16[64,16,1024]{2,1,0:T(8,128)(2,1)S(1)} %convolution_convert_fusion) | data formatting | bytes 4194304 | tf_op jit(solution)/shard_map/convert_element_type | solution.py:31
  6.1 7.6 %all-to-all-start.2 = ((bf16[64,16,1024]{2,0,1:T(8,128)(2,1)}), bf16[64,16,1024]{2,0,1:T(8,128)(2,1)}, u32[]{:S(2)}, u32[]{:S(2)}) async-start(bf16[64,16,1024]{2,0,1:T(8,128)(2,1)} %copy.67), calls=%async_computation.2 | async-start | bytes 4194304 | tf_op jit(solution)/shard_map/all_to_all | solution.py:39
  13.8 0.8 convolution_convert_fusion.1
  14.6 2.5 %copy.64 = bf16[64,16,1024]{2,0,1:T(8,128)(2,1)} copy(bf16[64,16,1024]{2,1,0:T(8,128)(2,1)S(1)} %convolution_convert_fusion.1) | data formatting | bytes 4194304 | tf_op jit(solution)/shard_map/convert_element_type | solution.py:37
  17.1 45.9 %all-to-all-done.2 = bf16[64,16,1024]{2,0,1:T(8,128)(2,1)} async-done(((bf16[64,16,1024]{2,0,1:T(8,128)(2,1)}), bf16[64,16,1024]{2,0,1:T(8,128)(2,1)}, u32[]{:S(2)}, u32[]{:S(2)}) %all-to-all-start.2) | async-done | bytes 2097184 | tf_op jit(solution)/shard_map/all_to_all | solution.py:39
  63.0 4.4 %all-to-all-start.1 = ((bf16[64,16,1024]{2,0,1:T(8,128)(2,1)}), bf16[64,16,1024]{2,0,1:T(8,128)(2,1)}, u32[]{:S(2)}, u32[]{:S(2)}) async-start(bf16[64,16,1024]{2,0,1:T(8,128)(2,1)} %copy.64), calls=%async_computation.1 | async-start | bytes 4194304 | tf_op jit(solution)/shard_map/all_to_all | solution.py:40
  67.5 2.7 %copy.68 = bf16[64,16,1024]{2,1,0:T(8,128)(2,1)S(1)} copy(bf16[64,16,1024]{2,0,1:T(8,128)(2,1)} %all-to-all-done.2) | data formatting | bytes 4194304 | tf_op jit(solution)/shard_map/all_to_all | solution.py:39
  70.3 1.4 copy-done.2
  71.6 3.5 %fusion.5 = f32[1024,768]{0,1:T(8,128)} fusion(bf16[1024,1024]{1,0:T(8,128)(2,1)S(1)} %bitcast.35, bf16[1,1024,768]{2,1,0:T(8,128)(2,1)S(1)} %copy-done), kind=kOutput, calls=%fused_computation.11 | convolution fusion | flops 1610612736 | bytes 6815744 | tf_op jit(solution)/shard_map/dot_general | solution.py:50
  75.1 41.7 %all-to-all-done.1 = bf16[64,16,1024]{2,0,1:T(8,128)(2,1)} async-done(((bf16[64,16,1024]{2,0,1:T(8,128)(2,1)}), bf16[64,16,1024]{2,0,1:T(8,128)(2,1)}, u32[]{:S(2)}, u32[]{:S(2)}) %all-to-all-start.1) | async-done | bytes 2097184 | tf_op jit(solution)/shard_map/all_to_all | solution.py:40
  116.8 2.9 %copy.65 = bf16[64,16,1024]{2,1,0:T(8,128)(2,1)S(1)} copy(bf16[64,16,1024]{2,0,1:T(8,128)(2,1)} %all-to-all-done.1) | data formatting | bytes 4194304 | tf_op jit(solution)/shard_map/all_to_all | solution.py:40
  119.8 2.1 multiply_reduce_fusion
  121.9 0.7 copy.72
  122.6 3.5 %all-to-all-start.4 = ((bf16[64,16,1]{0,2,1:T(2,128)(2,1)}), bf16[64,16,1]{0,2,1:T(2,128)(2,1)S(1)}, u32[]{:S(2)}, u32[]{:S(2)}) async-start(bf16[64,16,1]{0,2,1:T(2,128)(2,1)} %copy.72), calls=%async_computation.4 | async-start | bytes 16384 | tf_op jit(solution)/shard_map/all_to_all | solution.py:67
  126.1 0.1 copy.58
  126.3 6.1 %all-to-all-done.4 = bf16[64,16,1]{0,2,1:T(2,128)(2,1)S(1)} async-done(((bf16[64,16,1]{0,2,1:T(2,128)(2,1)}), bf16[64,16,1]{0,2,1:T(2,128)(2,1)S(1)}, u32[]{:S(2)}, u32[]{:S(2)}) %all-to-all-start.4) | async-done | bytes 2080 | tf_op jit(solution)/shard_map/all_to_all | solution.py:67
  132.5 9.0 %all_to_all.27 = bf16[64,16,1]{0,2,1:T(2,128)(2,1)S(1)} all-to-all(bf16[64,16,1]{0,2,1:T(2,128)(2,1)S(1)} %copy.60), channel_id=1, replica_groups=mesh['groups'=2,'replica'=1,'da'=4,'db'=4] {'da','db'}, dimensions={1} | all-to-all | bytes 4096 | tf_op jit(solution)/shard_map/all_to_all | solution.py:41
  141.6 2.8 %multiply_convert_fusion.4 = (bf16[1024,384]{0,1:T(8,128)(2,1)S(1)}, bf16[1024,384]{0,1:T(8,128)(2,1)S(1)}) fusion(f32[1024,768]{0,1:T(8,128)} %fusion.5, f32[1024,384]{0,1:T(8,128)S(1)} %get-tuple-element.30, f32[1024]{0:T(1024)S(1)} %reshape.93), kind=kLoop, calls=%fused_computation.16 | loop fusion | flops 5505024 | bytes 6295552 | tf_op jit(solution)/shard_map/convert.3
  144.4 1.9 convolution_convert_fusion.2
  146.3 2.5 %copy.69 = bf16[64,16,1024]{2,0,1:T(8,128)(2,1)} copy(bf16[64,16,1024]{2,1,0:T(8,128)(2,1)S(1)} %bitcast.39) | data formatting | bytes 4194304 | tf_op jit(solution)/shard_map/reshape | solution.py:63
  148.8 4.6 %all-to-all-start.3 = ((bf16[64,16,1024]{2,0,1:T(8,128)(2,1)}), bf16[64,16,1024]{2,0,1:T(8,128)(2,1)}, u32[]{:S(2)}, u32[]{:S(2)}) async-start(bf16[64,16,1024]{2,0,1:T(8,128)(2,1)} %copy.69), calls=%async_computation.3 | async-start | bytes 4194304 | tf_op jit(solution)/shard_map/all_to_all | solution.py:66
  153.4 0.1 copy.73
  153.5 0.7 copy.74
  154.2 3.7 %fusion.10 = bf16[1,384,1024]{2,1,0:T(8,128)(2,1)} fusion(bf16[1024,384]{0,1:T(8,128)(2,1)S(1)} %copy-done.12, bf16[1024,1024]{1,0:T(8,128)(2,1)} %bitcast.38, f32[1024]{0:T(1024)S(1)} %reshape.93), kind=kOutput, calls=%fused_computation.21 | convolution fusion | flops 808845312 | bytes 3674112 | tf_op jit(solution)/shard_map/rf,rd->fd/dot_general | solution.py:91
  157.9 3.0 %fusion.8 = bf16[1,1024,768]{2,1,0:T(8,128)(2,1)} fusion(bf16[1024,1024]{1,0:T(8,128)(2,1)S(1)} %bitcast.36, bf16[1024,384]{0,1:T(8,128)(2,1)S(1)} %copy-done.8, bf16[1024,384]{0,1:T(8,128)(2,1)S(1)} %copy-done.6), kind=kOutput, calls=%fused_computation.19 | convolution fusion | flops 1614544896 | bytes 5242880 | tf_op jit(solution)/shard_map/rd,rf->df/dot_general | solution.py:82
  160.9 41.9 %all-to-all-done.3 = bf16[64,16,1024]{2,0,1:T(8,128)(2,1)} async-done(((bf16[64,16,1024]{2,0,1:T(8,128)(2,1)}), bf16[64,16,1024]{2,0,1:T(8,128)(2,1)}, u32[]{:S(2)}, u32[]{:S(2)}) %all-to-all-start.3) | async-done | bytes 2097184 | tf_op jit(solution)/shard_map/all_to_all | solution.py:66
  202.8 2.9 %fusion.11 = bf16[64,2,1024]{2,1,0:T(2,128)(2,1)S(1)} fusion(pred[64,2,16]{2,1,0:T(4,128)(4,1)S(1)} %copy.70, bf16[64,16,1024]{2,0,1:T(8,128)(2,1)} %all-to-all-done.3), kind=kOutput, calls=%fused_computation.22 | convolution fusion | flops 4325376 | bytes 2361344 | tf_op jit(solution)/shard_map/rge,red->rgd/dot_general | solution.py:71
  205.7 0.8 reshape.91
  (36 shorter events, 0.6 us)
Async XLA Ops:
  0.6 71.0 %copy-start = (bf16[1,1024,768]{2,1,0:T(8,128)(2,1)S(1)}, bf16[1,1024,768]{2,1,0:T(8,128)(2,1)}, u32[]{:S(2)}) copy-start(bf16[1,1024,768]{2,1,0:T(8,128)(2,1)} %param.10) | copy-start | bytes 4718596
  6.1 7.6 %copy-start.9 = (bf16[128,1024]{1,0:T(8,128)(2,1)S(1)}, bf16[128,1024]{1,0:T(8,128)(2,1)}, u32[]{:S(2)}) copy-start(bf16[128,1024]{1,0:T(8,128)(2,1)} %param.7) | copy-start | bytes 786436
  6.1 56.9 %all-to-all-start.2 = ((bf16[64,16,1024]{2,0,1:T(8,128)(2,1)}), bf16[64,16,1024]{2,0,1:T(8,128)(2,1)}, u32[]{:S(2)}, u32[]{:S(2)}) async-start(bf16[64,16,1024]{2,0,1:T(8,128)(2,1)} %copy.67), calls=%async_computation.2 | async-start | bytes 4194304 | tf_op jit(solution)/shard_map/all_to_all | solution.py:39
  63.0 53.8 %all-to-all-start.1 = ((bf16[64,16,1024]{2,0,1:T(8,128)(2,1)}), bf16[64,16,1024]{2,0,1:T(8,128)(2,1)}, u32[]{:S(2)}, u32[]{:S(2)}) async-start(bf16[64,16,1024]{2,0,1:T(8,128)(2,1)} %copy.64), calls=%async_computation.1 | async-start | bytes 4194304 | tf_op jit(solution)/shard_map/all_to_all | solution.py:40
  70.2 1.4 copy-start.2
  116.8 2.9 %copy-start.1 = (f32[1024,768]{0,1:T(8,128)S(1)}, f32[1024,768]{0,1:T(8,128)}, u32[]{:S(2)}) copy-start(f32[1024,768]{0,1:T(8,128)} %fusion.5) | copy-start | bytes 9437188
  116.8 2.9 %copy-start.11 = (bf16[1,384,1024]{2,1,0:T(8,128)(2,1)S(1)}, bf16[1,384,1024]{2,1,0:T(8,128)(2,1)}, u32[]{:S(2)}) copy-start(bf16[1,384,1024]{2,1,0:T(8,128)(2,1)} %param.11) | copy-start | bytes 2359300
  119.7 2.1 %copy-start.4 = (bf16[64,16,1024]{2,1,0:T(8,128)(2,1)}, bf16[64,16,1024]{2,1,0:T(8,128)(2,1)S(1)}, u32[]{:S(2)}) copy-start(bf16[64,16,1024]{2,1,0:T(8,128)(2,1)S(1)} %copy.65) | copy-start | bytes 6291460
  119.8 6.3 %copy-start.10 = (bf16[128,8]{0,1:T(8,128)(2,1)S(1)}, bf16[128,8]{0,1:T(8,128)(2,1)}, u32[]{:S(2)}) copy-start(bf16[128,8]{0,1:T(8,128)(2,1)} %param.9) | copy-start | bytes 6148
  122.6 9.7 %all-to-all-start.4 = ((bf16[64,16,1]{0,2,1:T(2,128)(2,1)}), bf16[64,16,1]{0,2,1:T(2,128)(2,1)S(1)}, u32[]{:S(2)}, u32[]{:S(2)}) async-start(bf16[64,16,1]{0,2,1:T(2,128)(2,1)} %copy.72), calls=%async_computation.4 | async-start | bytes 16384 | tf_op jit(solution)/shard_map/all_to_all | solution.py:67
  144.4 1.9 copy-start.5
  144.4 1.9 copy-start.7
  148.8 5.3 %copy-start.12 = (bf16[1024,384]{0,1:T(8,128)(2,1)S(1)}, bf16[1024,384]{0,1:T(8,128)(2,1)}, u32[]{:S(2)}) copy-start(bf16[1024,384]{0,1:T(8,128)(2,1)} %get-tuple-element.27) | copy-start | bytes 2359300
  148.8 53.9 %all-to-all-start.3 = ((bf16[64,16,1024]{2,0,1:T(8,128)(2,1)}), bf16[64,16,1024]{2,0,1:T(8,128)(2,1)}, u32[]{:S(2)}, u32[]{:S(2)}) async-start(bf16[64,16,1024]{2,0,1:T(8,128)(2,1)} %copy.69), calls=%async_computation.3 | async-start | bytes 4194304 | tf_op jit(solution)/shard_map/all_to_all | solution.py:66
  154.2 3.7 %copy-start.3 = (bf16[64,16,1024]{2,1,0:T(8,128)(2,1)S(1)}, bf16[64,16,1024]{2,1,0:T(8,128)(2,1)}, u32[]{:S(2)}) copy-start(bf16[64,16,1024]{2,1,0:T(8,128)(2,1)} %copy-done.2) | copy-start | bytes 6291460
  154.2 3.7 %copy-start.6 = (bf16[1024,384]{0,1:T(8,128)(2,1)S(1)}, bf16[1024,384]{0,1:T(8,128)(2,1)}, u32[]{:S(2)}) copy-start(bf16[1024,384]{0,1:T(8,128)(2,1)} %copy-done.5) | copy-start | bytes 2359300
  154.2 3.7 %copy-start.8 = (bf16[1024,384]{0,1:T(8,128)(2,1)S(1)}, bf16[1024,384]{0,1:T(8,128)(2,1)}, u32[]{:S(2)}) copy-start(bf16[1024,384]{0,1:T(8,128)(2,1)} %copy-done.7) | copy-start | bytes 2359300
where the time goes:
time: 207 us; the launch traced here: 206 us
  waiting for transfers between devices  136 us (66%)
  starting transfers between devices  20.1 us (10%)
  local copies, waits for them, and re-layouts  19.5 us (9%)
  matrix products  18.6 us (9%)
  blocking collectives  8.95 us (4%)
  other arithmetic  2.92 us (1%)
    all_to_all x1, waiting for transfers between devices, body(): lax.all_to_all(input_send, ('da', 'db'), split_axis=1, concat_axis=1, til...  45.9 us
    all_to_all x1, waiting for transfers between devices, body(): lax.all_to_all(input_grads, ('da', 'db'), split_axis=1, concat_axis=1, ti...  41.9 us
    all_to_all x1, waiting for transfers between devices, body(): lax.all_to_all(upstream_send, ('da', 'db'), split_axis=1, concat_axis=1,...  41.7 us
    all_to_all x1, blocking collectives, body(): lax.all_to_all(gate_table, ('da', 'db'), split_axis=1, concat_axis=1, til...  8.95 us
    all_to_all x1, starting transfers between devices, body(): lax.all_to_all(input_send, ('da', 'db'), split_axis=1, concat_axis=1, til...  7.57 us
    all_to_all x1, waiting for transfers between devices, body(): lax.all_to_all(score_back, ('da', 'db'), split_axis=1, concat_axis=1, til...  6.08 us
    all_to_all x1, starting transfers between devices, body(): lax.all_to_all(input_grads, ('da', 'db'), split_axis=1, concat_axis=1, ti...  4.57 us
    all_to_all x1, starting transfers between devices, body(): lax.all_to_all(upstream_send, ('da', 'db'), split_axis=1, concat_axis=1,...  4.44 us
  transfers between devices with their start and end apart: 4, of which 4 were waited for; matrix products, arithmetic and copies ran while one was open for 8% of the time, Pallas kernels for 0%

commit v1 on v0

--- a/solution.py
+++ b/solution.py
@@ -63,7 +63,15 @@
     input_grads = input_grads.astype(jnp.bfloat16).reshape(rounds, experts, features)
     score_back = gate_scores.reshape(rounds, experts)
     returned, score_ret = (
-        lax.all_to_all(input_grads, ("da", "db"), split_axis=1, concat_axis=1, tiled=True),
+        jnp.concatenate(
+            lax.all_to_all(
+                jnp.stack(jnp.split(input_grads, lax.axis_size(("da", "db")), axis=1)),
+                ("da", "db"),
+                0,
+                0,
+            ),
+            axis=1,
+        ),
         lax.all_to_all(score_back, ("da", "db"), split_axis=1, concat_axis=1, tiled=True),
     )
     score_ret = score_ret.reshape(rounds, 1, 1, experts).astype(jnp.float32)

time: 207 us -> 220 us (1.063)
  local copies, waits for them, and re-layouts: 19.5 us -> 32.6 us
    unnamed x28 -> x43, local copies, waits for them, and re-layouts: 2.97 us -> 13.4 us
    split x0 -> x1, local copies, waits for them, and re-layouts: none -> 4.5 us  [body(): jnp.split(input_grads, lax.axis_size(('da', 'db')), axis=1)]
    reshape x1 -> x0, local copies, waits for them, and re-layouts: 2.51 us -> none  [body(): input_grads.astype(jnp.bfloat16).reshape(rounds, experts, features)]
where the time goes in v1:
time: 220 us
  waiting for transfers between devices  136 us (62%)
  local copies, waits for them, and re-layouts  32.6 us (15%)
  starting transfers between devices  20 us (9%)
  matrix products  18.6 us (8%)
  blocking collectives  8.95 us (4%)
  other arithmetic  2.92 us (1%)
    all_to_all x1, waiting for transfers between devices, body(): lax.all_to_all(input_send, ('da', 'db'), split_axis=1, concat_axis=1, til...  45.9 us
    all_to_all x1, waiting for transfers between devices, body(): lax.all_to_all(jnp.stack(jnp.split(input_grads, lax.axis_size(('da', 'db'...  41.9 us
    all_to_all x1, waiting for transfers between devices, body(): lax.all_to_all(upstream_send, ('da', 'db'), split_axis=1, concat_axis=1,...  41.7 us
    unnamed x43, local copies, waits for them, and re-layouts  13.4 us
    all_to_all x1, blocking collectives, body(): lax.all_to_all(gate_table, ('da', 'db'), split_axis=1, concat_axis=1, til...  8.95 us
    all_to_all x1, starting transfers between devices, body(): lax.all_to_all(input_send, ('da', 'db'), split_axis=1, concat_axis=1, til...  7.57 us
    all_to_all x1, waiting for transfers between devices, body(): lax.all_to_all(score_back, ('da', 'db'), split_axis=1, concat_axis=1, til...  6.08 us
    all_to_all x1, starting transfers between devices, body(): lax.all_to_all(jnp.stack(jnp.split(input_grads, lax.axis_size(('da', 'db'...  4.57 us
  transfers between devices with their start and end apart: 4, of which 4 were waited for; matrix products, arithmetic and copies ran while one was open for 8% of the time, Pallas kernels for 0%

profile of v1, /device:TPU:0, one launch (start us, length us, event | category | flops | bytes accessed | tf_op | source)
XLA Modules:
  0.0 219.6 jit_solution(4561392553299459852)
XLA Ops:
  0.6 0.9 copy.149
  1.8 1.1 reshape.94
  2.8 0.8 convolution_convert_fusion
  3.6 2.5 %copy.160 = bf16[64,16,1024]{2,0,1:T(8,128)(2,1)} copy(bf16[64,16,1024]{2,1,0:T(8,128)(2,1)S(1)} %convolution_convert_fusion) | data formatting | bytes 4194304 | tf_op jit(solution)/shard_map/convert_element_type | solution.py:31
  6.1 7.6 %all-to-all-start.2 = ((bf16[64,16,1024]{2,0,1:T(8,128)(2,1)}), bf16[64,16,1024]{2,0,1:T(8,128)(2,1)}, u32[]{:S(2)}, u32[]{:S(2)}) async-start(bf16[64,16,1024]{2,0,1:T(8,128)(2,1)} %copy.160), calls=%async_computation.2 | async-start | bytes 4194304 | tf_op jit(solution)/shard_map/all_to_all | solution.py:39
  13.8 0.8 convolution_convert_fusion.1
  14.6 2.5 %copy.157 = bf16[64,16,1024]{2,0,1:T(8,128)(2,1)} copy(bf16[64,16,1024]{2,1,0:T(8,128)(2,1)S(1)} %convolution_convert_fusion.1) | data formatting | bytes 4194304 | tf_op jit(solution)/shard_map/convert_element_type | solution.py:37
  17.1 45.9 %all-to-all-done.2 = bf16[64,16,1024]{2,0,1:T(8,128)(2,1)} async-done(((bf16[64,16,1024]{2,0,1:T(8,128)(2,1)}), bf16[64,16,1024]{2,0,1:T(8,128)(2,1)}, u32[]{:S(2)}, u32[]{:S(2)}) %all-to-all-start.2) | async-done | bytes 2097184 | tf_op jit(solution)/shard_map/all_to_all | solution.py:39
  63.0 4.4 %all-to-all-start.1 = ((bf16[64,16,1024]{2,0,1:T(8,128)(2,1)}), bf16[64,16,1024]{2,0,1:T(8,128)(2,1)}, u32[]{:S(2)}, u32[]{:S(2)}) async-start(bf16[64,16,1024]{2,0,1:T(8,128)(2,1)} %copy.157), calls=%async_computation.1 | async-start | bytes 4194304 | tf_op jit(solution)/shard_map/all_to_all | solution.py:40
  67.5 2.7 %copy.161 = bf16[64,16,1024]{2,1,0:T(8,128)(2,1)S(1)} copy(bf16[64,16,1024]{2,0,1:T(8,128)(2,1)} %all-to-all-done.2) | data formatting | bytes 4194304 | tf_op jit(solution)/shard_map/all_to_all | solution.py:39
  70.2 1.4 copy-done.2
  71.6 3.5 %fusion.6 = f32[1024,768]{0,1:T(8,128)} fusion(bf16[1024,1024]{1,0:T(8,128)(2,1)S(1)} %bitcast.107, bf16[1,1024,768]{2,1,0:T(8,128)(2,1)S(1)} %copy-done), kind=kOutput, calls=%fused_computation.12 | convolution fusion | flops 1610612736 | bytes 6815744 | tf_op jit(solution)/shard_map/dot_general | solution.py:50
  75.1 41.7 %all-to-all-done.1 = bf16[64,16,1024]{2,0,1:T(8,128)(2,1)} async-done(((bf16[64,16,1024]{2,0,1:T(8,128)(2,1)}), bf16[64,16,1024]{2,0,1:T(8,128)(2,1)}, u32[]{:S(2)}, u32[]{:S(2)}) %all-to-all-start.1) | async-done | bytes 2097184 | tf_op jit(solution)/shard_map/all_to_all | solution.py:40
  116.8 2.9 %copy.158 = bf16[64,16,1024]{2,1,0:T(8,128)(2,1)S(1)} copy(bf16[64,16,1024]{2,0,1:T(8,128)(2,1)} %all-to-all-done.1) | data formatting | bytes 4194304 | tf_op jit(solution)/shard_map/all_to_all | solution.py:40
  119.8 2.1 multiply_reduce_fusion
  122.6 3.5 %all-to-all-start.4 = ((bf16[64,16,1]{0,2,1:T(2,128)(2,1)}), bf16[64,16,1]{0,2,1:T(2,128)(2,1)S(1)}, u32[]{:S(2)}, u32[]{:S(2)}) async-start(bf16[64,16,1]{0,2,1:T(2,128)(2,1)} %copy.180), calls=%async_computation.4 | async-start | bytes 16384 | tf_op jit(solution)/shard_map/all_to_all | solution.py:75
  126.3 6.1 %all-to-all-done.4 = bf16[64,16,1]{0,2,1:T(2,128)(2,1)S(1)} async-done(((bf16[64,16,1]{0,2,1:T(2,128)(2,1)}), bf16[64,16,1]{0,2,1:T(2,128)(2,1)S(1)}, u32[]{:S(2)}, u32[]{:S(2)}) %all-to-all-start.4) | async-done | bytes 2080 | tf_op jit(solution)/shard_map/all_to_all | solution.py:75
  132.4 9.0 %all_to_all.27 = bf16[64,16,1]{0,2,1:T(2,128)(2,1)S(1)} all-to-all(bf16[64,16,1]{0,2,1:T(2,128)(2,1)S(1)} %copy.153), channel_id=1, replica_groups=mesh['groups'=2,'replica'=1,'da'=4,'db'=4] {'da','db'}, dimensions={1} | all-to-all | bytes 4096 | tf_op jit(solution)/shard_map/all_to_all | solution.py:41
  141.6 2.8 %multiply_convert_fusion.4 = (bf16[1024,384]{0,1:T(8,128)(2,1)S(1)}, bf16[1024,384]{0,1:T(8,128)(2,1)S(1)}) fusion(f32[1024,768]{0,1:T(8,128)} %fusion.6, f32[1024,384]{0,1:T(8,128)S(1)} %get-tuple-element.46, f32[1024]{0:T(1024)S(1)} %reshape.101), kind=kLoop, calls=%fused_computation.17 | loop fusion | flops 5505024 | bytes 6295552 | tf_op jit(solution)/shard_map/convert.3
  144.4 1.9 convolution_convert_fusion.2
  146.3 4.5 %fusion.36 = (bf16[64,1,1024]{2,1,0:T(2,128)(2,1)S(1)}, bf16[64,1,1024]{2,1,0:T(2,128)(2,1)S(1)}, bf16[64,1,1024]{2,1,0:T(2,128)(2,1)S(1)}, bf16[64,1,1024]{2,1,...) fusion(bf16[64,16,1024]{2,1,0:T(8,128)(2,1)S(1)} %bitcast.106), kind=kLoop, calls=%fused_computation.66 | loop fusion | bytes 4194304 | tf_op jit(solution)/shard_map/split | solution.py:68
  154.3 0.7 fusion.27
  155.0 0.7 fusion.26
  156.4 0.7 fusion.24
  159.2 0.7 fusion.20
  159.9 0.7 fusion.19
  162.0 4.6 %all-to-all-start.3 = ((bf16[16,64,1,1024]{3,1,2,0:T(8,128)(2,1)}), bf16[16,64,1,1024]{3,1,2,0:T(8,128)(2,1)}, u32[]{:S(2)}, u32[]{:S(2)}) async-start(bf16[16,64,1,1024]{3,1,2,0:T(8,128)(2,1)} %fusion.17), calls=%async_computation.3 | async-start | bytes 4194304 | tf_op jit(solution)/shard_map/all_to_all | solution.py:67
  167.3 3.7 %fusion.11 = bf16[1,384,1024]{2,1,0:T(8,128)(2,1)} fusion(bf16[1024,384]{0,1:T(8,128)(2,1)S(1)} %copy-done.12, bf16[1024,1024]{1,0:T(8,128)(2,1)} %bitcast.110, f32[1024]{0:T(1024)S(1)} %reshape.101), kind=kOutput, calls=%fused_computation.22 | convolution fusion | flops 808845312 | bytes 3674112 | tf_op jit(solution)/shard_map/rf,rd->fd/dot_general | solution.py:99
  171.0 3.0 %fusion.9 = bf16[1,1024,768]{2,1,0:T(8,128)(2,1)} fusion(bf16[1024,1024]{1,0:T(8,128)(2,1)S(1)} %bitcast.108, bf16[1024,384]{0,1:T(8,128)(2,1)S(1)} %copy-done.8, bf16[1024,384]{0,1:T(8,128)(2,1)S(1)} %copy-done.6), kind=kOutput, calls=%fused_computation.20 | convolution fusion | flops 1614544896 | bytes 5242880 | tf_op jit(solution)/shard_map/rd,rf->df/dot_general | solution.py:90
  174.0 41.9 %all-to-all-done.3 = bf16[16,64,1,1024]{3,1,2,0:T(8,128)(2,1)} async-done(((bf16[16,64,1,1024]{3,1,2,0:T(8,128)(2,1)}), bf16[16,64,1,1024]{3,1,2,0:T(8,128)(2,1)}, u32[]{:S(2)}, u32[]{:S(2)}) %all-to-all-start.3) | async-done | bytes 2097184 | tf_op jit(solution)/shard_map/all_to_all | solution.py:67
  215.9 2.9 %fusion.12 = bf16[64,2,1024]{2,1,0:T(2,128)(2,1)S(1)} fusion(pred[64,2,16]{2,1,0:T(4,128)(4,1)S(1)} %copy.179, bf16[16,64,1,1024]{3,1,2,0:T(8,128)(2,1)} %all-to-all-done.3), kind=kOutput, calls=%fused_computation.23 | convolution fusion | flops 4325376 | bytes 2361344 | tf_op jit(solution)/shard_map/rge,red->rgd/dot_general | solution.py:79
  218.8 0.8 reshape.99
  (52 shorter events, 9.9 us)
Async XLA Ops:
  0.6 71.0 %copy-start = (bf16[1,1024,768]{2,1,0:T(8,128)(2,1)S(1)}, bf16[1,1024,768]{2,1,0:T(8,128)(2,1)}, u32[]{:S(2)}) copy-start(bf16[1,1024,768]{2,1,0:T(8,128)(2,1)} %param.10) | copy-start | bytes 4718596
  6.1 7.6 %copy-start.9 = (bf16[128,1024]{1,0:T(8,128)(2,1)S(1)}, bf16[128,1024]{1,0:T(8,128)(2,1)}, u32[]{:S(2)}) copy-start(bf16[128,1024]{1,0:T(8,128)(2,1)} %param.7) | copy-start | bytes 786436
  6.1 56.9 %all-to-all-start.2 = ((bf16[64,16,1024]{2,0,1:T(8,128)(2,1)}), bf16[64,16,1024]{2,0,1:T(8,128)(2,1)}, u32[]{:S(2)}, u32[]{:S(2)}) async-start(bf16[64,16,1024]{2,0,1:T(8,128)(2,1)} %copy.160), calls=%async_computation.2 | async-start | bytes 4194304 | tf_op jit(solution)/shard_map/all_to_all | solution.py:39
  63.0 53.8 %all-to-all-start.1 = ((bf16[64,16,1024]{2,0,1:T(8,128)(2,1)}), bf16[64,16,1024]{2,0,1:T(8,128)(2,1)}, u32[]{:S(2)}, u32[]{:S(2)}) async-start(bf16[64,16,1024]{2,0,1:T(8,128)(2,1)} %copy.157), calls=%async_computation.1 | async-start | bytes 4194304 | tf_op jit(solution)/shard_map/all_to_all | solution.py:40
  70.2 1.4 copy-start.2
  116.8 2.9 %copy-start.1 = (f32[1024,768]{0,1:T(8,128)S(1)}, f32[1024,768]{0,1:T(8,128)}, u32[]{:S(2)}) copy-start(f32[1024,768]{0,1:T(8,128)} %fusion.6) | copy-start | bytes 9437188
  116.8 2.9 %copy-start.11 = (bf16[1,384,1024]{2,1,0:T(8,128)(2,1)S(1)}, bf16[1,384,1024]{2,1,0:T(8,128)(2,1)}, u32[]{:S(2)}) copy-start(bf16[1,384,1024]{2,1,0:T(8,128)(2,1)} %param.11) | copy-start | bytes 2359300
  119.7 2.1 copy-start.4
  119.8 6.3 %copy-start.10 = (bf16[128,8]{0,1:T(8,128)(2,1)S(1)}, bf16[128,8]{0,1:T(8,128)(2,1)}, u32[]{:S(2)}) copy-start(bf16[128,8]{0,1:T(8,128)(2,1)} %param.9) | copy-start | bytes 6148
  122.6 9.7 %all-to-all-start.4 = ((bf16[64,16,1]{0,2,1:T(2,128)(2,1)}), bf16[64,16,1]{0,2,1:T(2,128)(2,1)S(1)}, u32[]{:S(2)}, u32[]{:S(2)}) async-start(bf16[64,16,1]{0,2,1:T(2,128)(2,1)} %copy.180), calls=%async_computation.4 | async-start | bytes 16384 | tf_op jit(solution)/shard_map/all_to_all | solution.py:75
  144.4 1.9 copy-start.5
  144.4 1.9 copy-start.7
  162.0 5.3 %copy-start.12 = (bf16[1024,384]{0,1:T(8,128)(2,1)S(1)}, bf16[1024,384]{0,1:T(8,128)(2,1)}, u32[]{:S(2)}) copy-start(bf16[1024,384]{0,1:T(8,128)(2,1)} %get-tuple-element.27) | copy-start | bytes 2359300
  162.0 53.9 %all-to-all-start.3 = ((bf16[16,64,1,1024]{3,1,2,0:T(8,128)(2,1)}), bf16[16,64,1,1024]{3,1,2,0:T(8,128)(2,1)}, u32[]{:S(2)}, u32[]{:S(2)}) async-start(bf16[16,64,1,1024]{3,1,2,0:T(8,128)(2,1)} %fusion.17), calls=%async_computation.3 | async-start | bytes 4194304 | tf_op jit(solution)/shard_map/all_to_all | solution.py:67
  167.3 3.7 %copy-start.3 = (bf16[64,16,1024]{2,1,0:T(8,128)(2,1)S(1)}, bf16[64,16,1024]{2,1,0:T(8,128)(2,1)}, u32[]{:S(2)}) copy-start(bf16[64,16,1024]{2,1,0:T(8,128)(2,1)} %copy-done.2) | copy-start | bytes 6291460
  167.3 3.7 %copy-start.6 = (bf16[1024,384]{0,1:T(8,128)(2,1)S(1)}, bf16[1024,384]{0,1:T(8,128)(2,1)}, u32[]{:S(2)}) copy-start(bf16[1024,384]{0,1:T(8,128)(2,1)} %copy-done.5) | copy-start | bytes 2359300
  167.3 3.7 %copy-start.8 = (bf16[1024,384]{0,1:T(8,128)(2,1)S(1)}, bf16[1024,384]{0,1:T(8,128)(2,1)}, u32[]{:S(2)}) copy-start(bf16[1024,384]{0,1:T(8,128)(2,1)} %copy-done.7) | copy-start | bytes 2359300
